TPU v7x, 32 devices: a whole 2x2x4 slice. The times are simulated.
32 devices in a mesh: grp: 2 (over x), blk: 8 (over z, y), sub: 2 (over core).
Axes of the slice: x: 2, y: 2, z: 4, core: 2. Of those that a mesh axis runs over, the one named last changes fastest.
Arguments:
- spectra: bfloat16 [16, 2, 256, 2048], P('sub', None, None, ('grp', 'blk')), parts along dimension 3, may hold values from -6 to 6
- direction: int32 [2, 8], P(None, 'blk'), may hold values 0 or 1
Outputs:
- correlations: float32 [2, 16, 64, 128, 128], P(None, ('grp', 'blk'), 'sub'), parts along dimension 1
There are 2 independent parts, one for each index of `grp`. A program takes and returns all parts, laid end to end along the dimension named above; an argument that names none is the same for every part. Nothing has to cross between parts.
Inputs may be any that keep to these rules, and one draw needn't show every extreme that they name: direction[r, b] = 1 puts block b's partner in round r at block b + r + 1, 0 at block b - r - 1, modulo 8.
All inputs are finite; a program needn't handle non-finite values.
Results may differ from a plain program's by a relative error of at most 0.011.
Values may be sent and summed in bfloat16 or wider, within the bound.
A program may use at most 128 MiB of HBM per device.

v0:
```python
import math

import jax
import jax.numpy as jnp
from jax import lax
from jax.sharding import PartitionSpec as P

LAGS = 64
ROUNDS = 2


def from_behind(x, axis, by):
    size = lax.axis_size(axis)
    return lax.ppermute(x, axis, [(i, (i + by) % size) for i in range(size)])


def make_table(bin_count, windows, lag_count):
    lags = jnp.arange(lag_count, dtype=jnp.int32) - lag_count // 2
    bins = jnp.arange(bin_count, dtype=jnp.int32)
    period = 2 * bin_count
    phase = bins[None, :] * ((lags[:, None] + period) % period) % period
    angle = phase.astype(jnp.float32) * (math.pi / bin_count)
    weight = (bin_count * windows) ** (-0.5)
    return (jnp.stack([jnp.cos(angle), -jnp.sin(angle)], axis=-1) * weight).astype(jnp.bfloat16)


def correlate(local_block, partner, lag_table):
    windows, _, bin_count, channels = local_block.shape
    swapped = jnp.stack([partner[:, 1], -partner[:, 0]], axis=1)
    operand = jnp.concatenate([partner, swapped], axis=-1)
    bin_block = min(128, bin_count)
    summed = jnp.zeros((lag_table.shape[0], channels, channels), jnp.float32)
    for first_bin in range(0, bin_count, bin_block):
        left_part = local_block[:, :, first_bin : first_bin + bin_block]
        right_part = operand[:, :, first_bin : first_bin + bin_block]
        cross_tile = jnp.einsum(
            "scfi,scfj->fij", left_part, right_part, preferred_element_type=jnp.bfloat16
        )
        cross_tile = cross_tile.reshape(bin_block, channels, 2, channels)
        table_part = lag_table[:, first_bin : first_bin + bin_block]
        summed = summed + jnp.einsum(
            "tfk,fikj->tij", table_part, cross_tile, preferred_element_type=jnp.float32
        )
    return summed


def per_device(spectra, direction):
    windows, _, bin_count, channels = spectra.shape
    lag_table = make_table(bin_count, windows * lax.axis_size("sub"), LAGS)
    ahead = spectra
    behind = spectra
    reduced_rounds = []
    for round_index in range(ROUNDS):
        ahead = from_behind(spectra, "blk", -(round_index + 1))
        behind = from_behind(spectra, "blk", round_index + 1)
        partner = jnp.where(direction[round_index, 0] == 1, ahead, behind)
        partial_lags = correlate(spectra, partner, lag_table)
        reduced_rounds.append(
            lax.psum_scatter(
                partial_lags.astype(jnp.bfloat16), "sub", scatter_dimension=0, tiled=True
            ).astype(jnp.float32)
        )
    reduced = jnp.stack(reduced_rounds, axis=0)
    return reduced[:, None]


def solution(mesh):
    return jax.shard_map(
        per_device,
        mesh=mesh,
        in_specs=(P("sub", None, None, ("grp", "blk")), P(None, "blk")),
        out_specs=P(None, ("grp", "blk"), "sub", None, None),
        check_vma=False,
    )
```

profile of v0, /device:TPU:0, one launch (start us, length us, event | category | flops | bytes accessed | tf_op | source)
XLA Modules:
  0.0 180.7 jit_solution(10108547325119340823)
XLA Ops:
  6.5 0.0 reduce-scatter.5.cloned.1.call-start
  6.5 3.0 %copy.3 = bf16[8,2,256,128]{3,0,1,2:T(8,128)(2,1)} copy(bf16[8,2,256,128]{3,2,1,0:T(8,128)(2,1)} %param.2) | data formatting | bytes 2097152 | tf_op args[0]
  9.5 5.1 %collective-permute-start.2 = (bf16[8,2,256,128]{3,0,1,2:T(8,128)(2,1)}, bf16[8,2,256,128]{3,0,1,2:T(8,128)(2,1)S(1)}, u32[]{:S(2)}, u32[]{:S(2)}) collective-permute-start(bf16[8,2,256,128]{3,0,1,2:T(8,128)(2,1)} %copy.3), channel_id=1, source_target_pairs={{0,12},{2,14},{4,0},{6,2},{8,4},{10,6},{12,8},{14,10},{1,13},{3,15... | collective-permute-start | bytes 3145736 | tf_op jit(solution)/shard_map/ppermute | solution.py:14
  14.6 0.0 collective-permute-start.3
  14.6 4.8 %collective-permute-start = (bf16[8,2,256,128]{3,0,1,2:T(8,128)(2,1)}, bf16[8,2,256,128]{3,0,1,2:T(8,128)(2,1)}, u32[]{:S(2)}, u32[]{:S(2)}) collective-permute-start(bf16[8,2,256,128]{3,0,1,2:T(8,128)(2,1)} %copy.3), channel_id=1, source_target_pairs={{0,14},{2,0},{4,2},{6,4},{8,6},{10,8},{12,10},{14,12},{1,15},{3,1}... | collective-permute-start | bytes 3145736 | tf_op jit(solution)/shard_map/ppermute | solution.py:14
  19.4 0.0 collective-permute-start.1
  19.4 0.3 fusion.18
  19.7 0.6 fusion.11
  20.3 1.4 fusion.28
  23.0 1.1 fusion.41
  24.1 1.9 %fusion.39 = bf16[8,2,128,128]{3,0,1,2:T(8,128)(2,1)} fusion(bf16[8,2,256,128]{3,0,1,2:T(8,128)(2,1)} %copy.3), kind=kLoop, calls=%fused_computation.16.clone.2 | loop fusion | bytes 1048576 | tf_op jit(solution)/shard_map/scfi,scfj->fij/dot_general | solution.py:36
  25.9 1.9 %fusion.45 = bf16[8,2,128,128]{3,0,1,2:T(8,128)(2,1)} fusion(bf16[8,2,256,128]{3,0,1,2:T(8,128)(2,1)} %copy.3), kind=kLoop, calls=%fused_computation.19.clone | loop fusion | bytes 1048576 | tf_op jit(solution)/shard_map/scfi,scfj->fij/dot_general | solution.py:36
  27.8 1.9 %fusion.43 = bf16[8,2,128,128]{3,0,1,2:T(8,128)(2,1)} fusion(bf16[8,2,256,128]{3,0,1,2:T(8,128)(2,1)} %copy.3), kind=kLoop, calls=%fused_computation.17.clone | loop fusion | bytes 1048576 | tf_op jit(solution)/shard_map/scfi,scfj->fij/dot_general | solution.py:36
  29.7 8.7 %collective-permute-done.2 = bf16[8,2,256,128]{3,0,1,2:T(8,128)(2,1)S(1)} collective-permute-done((bf16[8,2,256,128]{3,0,1,2:T(8,128)(2,1)}, bf16[8,2,256,128]{3,0,1,2:T(8,128)(2,1)S(1)}, u32[]{:S(2)}, u32[]{:S(2)}) %collective-permute-start.2) | collective-permute-done | bytes 1048608 | tf_op jit(solution)/shard_map/ppermute | solution.py:14
  38.4 23.3 %collective-permute-done.3 = bf16[8,2,256,128]{3,0,1,2:T(8,128)(2,1)S(1)} collective-permute-done((bf16[8,2,256,128]{3,0,1,2:T(8,128)(2,1)}, bf16[8,2,256,128]{3,0,1,2:T(8,128)(2,1)S(1)}, u32[]{:S(2)}, u32[]{:S(2)}) %collective-permute-start.3) | collective-permute-done | bytes 1048608 | tf_op jit(solution)/shard_map/ppermute | solution.py:14
  61.8 0.1 broadcast_select_fusion
  61.9 0.1 fusion.27
  62.0 6.8 %fusion.4 = bf16[128,256,128,1]{2,1,3,0:T(8,128)(2,1)} fusion(bf16[8,1,256,128]{3,0,1,2:T(8,128)(2,1)S(1)} %get-tuple-element.8, bf16[8,1,256,128]{3,0,1,2:T(8,128)(2,1)S(1)} %get-tuple-element.7, bf16[8,2,256,128]{3,0,1,2:T(8,128)(2,1)S(1)} %broadcast_select_fusion, bf16[8,2,128,128]{3,0,1,2:T(8,128)(2,1)S(1)} %fusion.41), kind=kOutput, calls=%fused_computation.11 | convolution fusion | flops 140509184 | bytes 11010048 | tf_op jit(solution)/shard_map/scfi,scfj->fij/dot_general | solution.py:36
  68.9 0.0 copy-start.6
  68.9 12.4 %copy.11 = bf16[128,128,2,128]{3,0,2,1:T(8,128)(2,1)} copy(bf16[128,128,2,128]{1,3,2,0:T(8,128)(2,1)} %bitcast.68) | data formatting | bytes 16777216 | tf_op jit(solution)/shard_map/reshape | solution.py:39
  81.2 0.0 copy-done.6
  81.2 6.8 %fusion.3 = bf16[128,256,128,1]{2,1,3,0:T(8,128)(2,1)} fusion(bf16[8,1,256,128]{3,0,1,2:T(8,128)(2,1)S(1)} %get-tuple-element.8, bf16[8,1,256,128]{3,0,1,2:T(8,128)(2,1)S(1)} %get-tuple-element.7, bf16[8,2,256,128]{3,0,1,2:T(8,128)(2,1)S(1)} %broadcast_select_fusion, bf16[8,2,128,128]{3,0,1,2:T(8,128)(2,1)S(1)} %copy-done.6), kind=kOutput, calls=%fused_computation.10 | convolution fusion | flops 140509184 | bytes 11010048 | tf_op jit(solution)/shard_map/scfi,scfj->fij/dot_general | solution.py:36
  88.1 0.0 copy-start.2
  88.1 12.4 %copy.12 = bf16[128,128,2,128]{3,0,2,1:T(8,128)(2,1)} copy(bf16[128,128,2,128]{1,3,2,0:T(8,128)(2,1)} %bitcast.67) | data formatting | bytes 16777216 | tf_op jit(solution)/shard_map/reshape | solution.py:39
  100.5 0.0 copy-done.2
  100.5 0.0 copy-start.1
  100.5 5.1 %fusion.19 = f32[64,128,128,1]{2,0,3,1:T(8,128)S(1)} fusion(bf16[128,128,2,128]{3,0,2,1:T(8,128)(2,1)} %copy.11, bf16[64,256,2]{1,0,2:T(8,128)(2,1)S(1)} %copy-done.2), kind=kOutput, calls=%fused_computation.35 | convolution fusion | flops 536870912 | bytes 12615680 | tf_op jit(solution)/shard_map/tfk,fikj->tij/dot_general | solution.py:41
  105.6 0.7 copy-done.1
  106.3 2.9 %fusion = bf16[64,128,128]{2,0,1:T(8,128)(2,1)} fusion(f32[64,128,128,1]{2,0,3,1:T(8,128)S(1)} %fusion.19, bf16[128,128,2,128]{3,0,2,1:T(8,128)(2,1)S(1)} %copy-done.1, bf16[64,256,2]{1,0,2:T(8,128)(2,1)S(1)} %copy-done.2), kind=kOutput, calls=%fused_computation.1 | convolution fusion | flops 538968064 | bytes 14712832 | tf_op jit(solution)/shard_map/tfk,fikj->tij/dot_general | solution.py:41
  109.2 0.0 copy-start.5
  109.2 0.0 reduce-scatter.5.cloned.1.call-update
  109.2 0.2 reduce-scatter.3.cloned.1.call-start
  109.5 0.0 collective-permute-done
  109.5 0.0 collective-permute-done.1
  109.5 1.3 broadcast_select_fusion.1
  110.8 0.1 fusion.26
  111.0 0.0 copy-done.5
  111.0 0.0 copy-start.4
  111.0 6.8 %fusion.6 = bf16[128,256,128,1]{2,1,3,0:T(8,128)(2,1)} fusion(bf16[8,1,256,128]{3,0,1,2:T(8,128)(2,1)S(1)} %get-tuple-element.6, bf16[8,1,256,128]{3,0,1,2:T(8,128)(2,1)S(1)} %get-tuple-element.5, bf16[8,2,256,128]{3,0,1,2:T(8,128)(2,1)S(1)} %broadcast_select_fusion.1, bf16[8,2,128,128]{3,0,1,2:T(8,128)(2,1)S(1)} %copy-done.5), kind=kOutput, calls=%fused_computation.13 | convolution fusion | flops 140509184 | bytes 11010048 | tf_op jit(solution)/shard_map/scfi,scfj->fij/dot_general | solution.py:36
  117.9 0.0 copy-done.4
  117.9 6.8 %fusion.5 = bf16[128,256,128,1]{2,1,3,0:T(8,128)(2,1)} fusion(bf16[8,1,256,128]{3,0,1,2:T(8,128)(2,1)S(1)} %get-tuple-element.6, bf16[8,1,256,128]{3,0,1,2:T(8,128)(2,1)S(1)} %get-tuple-element.5, bf16[8,2,256,128]{3,0,1,2:T(8,128)(2,1)S(1)} %broadcast_select_fusion.1, bf16[8,2,128,128]{3,0,1,2:T(8,128)(2,1)S(1)} %copy-done.4), kind=kOutput, calls=%fused_computation.12 | convolution fusion | flops 140509184 | bytes 11010048 | tf_op jit(solution)/shard_map/scfi,scfj->fij/dot_general | solution.py:36
  124.7 12.3 %copy.6 = bf16[128,128,2,128]{3,0,2,1:T(8,128)(2,1)} copy(bf16[128,128,2,128]{1,3,2,0:T(8,128)(2,1)} %bitcast.65) | data formatting | bytes 16777216 | tf_op jit(solution)/shard_map/reshape | solution.py:39
  137.0 0.0 copy-start.3
  137.0 12.4 %copy.8 = bf16[128,128,2,128]{3,0,2,1:T(8,128)(2,1)} copy(bf16[128,128,2,128]{1,3,2,0:T(8,128)(2,1)} %bitcast.66) | data formatting | bytes 16777216 | tf_op jit(solution)/shard_map/reshape | solution.py:39
  149.4 0.0 copy-done.3
  149.4 0.0 copy-start
  149.4 5.1 %fusion.20 = f32[64,128,128,1]{2,0,3,1:T(8,128)S(1)} fusion(bf16[128,128,2,128]{3,0,2,1:T(8,128)(2,1)} %copy.6, bf16[64,256,2]{1,0,2:T(8,128)(2,1)S(1)} %copy-done.3), kind=kOutput, calls=%fused_computation.36 | convolution fusion | flops 536870912 | bytes 12615680 | tf_op jit(solution)/shard_map/tfk,fikj->tij/dot_general | solution.py:41
  154.5 0.7 copy-done
  155.2 3.0 %fusion.1 = bf16[64,128,128]{2,0,1:T(8,128)(2,1)} fusion(f32[64,128,128,1]{2,0,3,1:T(8,128)S(1)} %fusion.20, bf16[128,128,2,128]{3,0,2,1:T(8,128)(2,1)S(1)} %copy-done, bf16[64,256,2]{1,0,2:T(8,128)(2,1)S(1)} %copy-done.3), kind=kOutput, calls=%fused_computation.3 | convolution fusion | flops 538968064 | bytes 14712832 | tf_op jit(solution)/shard_map/tfk,fikj->tij/dot_general | solution.py:41
  158.2 0.0 reduce-scatter.3.cloned.1.call-update
  158.2 0.0 reduce-scatter.5.cloned.1.call-done
  158.2 9.4 %reduce-scatter.3.cloned.1.call-done = bf16[32,128,128]{2,0,1:T(8,128)(2,1)} async-done(((bf16[64,128,128]{2,0,1:T(8,128)(2,1)}), bf16[32,128,128]{2,0,1:T(8,128)(2,1)}) %reduce-scatter.3.cloned.1.call-update) | async-done | bytes 1048592 | tf_op jit(solution)/shard_map/reduce_scatter | solution.py:59
  167.6 1.8 %fusion.2 = f32[2,1,32,128,128]{4,2,3,0,1:T(8,128)S(1)} fusion(bf16[1,32,128,128]{3,1,2,0:T(8,128)(2,1)} %bitcast.69, bf16[1,32,128,128]{3,1,2,0:T(8,128)(2,1)} %bitcast.70), kind=kLoop, calls=%fused_computation.7 | loop fusion | flops 2097152 | bytes 6291456 | tf_op jit(solution)/shard_map/broadcast_in_dim | solution.py:64
  169.4 4.4 %copy.13 = f32[2,1,32,128,128]{4,3,2,1,0:T(8,128)} copy(f32[2,1,32,128,128]{4,2,3,0,1:T(8,128)S(1)} %fusion.2) | data formatting | bytes 8388608 | tf_op jit(solution)/shard_map/broadcast_in_dim | solution.py:64
  (1 shorter events, 0.0 us)
Async XLA Ops:
  6.5 151.7 %reduce-scatter.5.cloned.1.call-start = ((), (), s32[]{:S(2)}) async-start(), calls=%async_computation.3 | async-start | bytes 3145728 | tf_op jit(solution)/shard_map/reduce_scatter | solution.py:59
  9.5 28.9 %collective-permute-start.2 = (bf16[8,2,256,128]{3,0,1,2:T(8,128)(2,1)}, bf16[8,2,256,128]{3,0,1,2:T(8,128)(2,1)S(1)}, u32[]{:S(2)}, u32[]{:S(2)}) collective-permute-start(bf16[8,2,256,128]{3,0,1,2:T(8,128)(2,1)} %copy.3), channel_id=1, source_target_pairs={{0,12},{2,14},{4,0},{6,2},{8,4},{10,6},{12,8},{14,10},{1,13},{3,15... | collective-permute-start | bytes 3145736 | tf_op jit(solution)/shard_map/ppermute | solution.py:14
  14.6 47.2 %collective-permute-start.3 = (bf16[8,2,256,128]{3,0,1,2:T(8,128)(2,1)}, bf16[8,2,256,128]{3,0,1,2:T(8,128)(2,1)S(1)}, u32[]{:S(2)}, u32[]{:S(2)}) collective-permute-start(bf16[8,2,256,128]{3,0,1,2:T(8,128)(2,1)} %copy.3), channel_id=1, source_target_pairs={{0,4},{2,6},{4,8},{6,10},{8,12},{10,14},{12,0},{14,2},{1,5},{3,7},... | collective-permute-start | bytes 3145736 | tf_op jit(solution)/shard_map/ppermute | solution.py:14
  14.6 94.9 %collective-permute-start = (bf16[8,2,256,128]{3,0,1,2:T(8,128)(2,1)}, bf16[8,2,256,128]{3,0,1,2:T(8,128)(2,1)}, u32[]{:S(2)}, u32[]{:S(2)}) collective-permute-start(bf16[8,2,256,128]{3,0,1,2:T(8,128)(2,1)} %copy.3), channel_id=1, source_target_pairs={{0,14},{2,0},{4,2},{6,4},{8,6},{10,8},{12,10},{14,12},{1,15},{3,1}... | collective-permute-start | bytes 3145736 | tf_op jit(solution)/shard_map/ppermute | solution.py:14
  19.4 90.1 %collective-permute-start.1 = (bf16[8,2,256,128]{3,0,1,2:T(8,128)(2,1)}, bf16[8,2,256,128]{3,0,1,2:T(8,128)(2,1)}, u32[]{:S(2)}, u32[]{:S(2)}) collective-permute-start(bf16[8,2,256,128]{3,0,1,2:T(8,128)(2,1)} %copy.3), channel_id=1, source_target_pairs={{0,2},{2,4},{4,6},{6,8},{8,10},{10,12},{12,14},{14,0},{1,3},{3,5},... | collective-permute-start | bytes 3145736 | tf_op jit(solution)/shard_map/ppermute | solution.py:14
  68.9 12.4 %copy-start.6 = (bf16[8,2,128,128]{3,0,1,2:T(8,128)(2,1)S(1)}, bf16[8,2,128,128]{3,0,1,2:T(8,128)(2,1)}, u32[]{:S(2)}) copy-start(bf16[8,2,128,128]{3,0,1,2:T(8,128)(2,1)} %fusion.39) | copy-start | bytes 1572868
  88.1 12.4 %copy-start.2 = (bf16[64,256,2]{1,0,2:T(8,128)(2,1)S(1)}, bf16[64,256,2]{1,0,2:T(8,128)(2,1)}, u32[]{:S(2)}) copy-start(bf16[64,256,2]{1,0,2:T(8,128)(2,1)} %fusion.11) | copy-start | bytes 196612
  100.5 5.8 %copy-start.1 = (bf16[128,128,2,128]{3,0,2,1:T(8,128)(2,1)S(1)}, bf16[128,128,2,128]{3,0,2,1:T(8,128)(2,1)}, u32[]{:S(2)}) copy-start(bf16[128,128,2,128]{3,0,2,1:T(8,128)(2,1)} %copy.12) | copy-start | bytes 25165828
  109.2 1.8 copy-start.5
  109.2 58.3 %reduce-scatter.3.cloned.1.call-start = ((), (), s32[]{:S(2)}) async-start(), calls=%async_computation.2 | async-start | bytes 3145728 | tf_op jit(solution)/shard_map/reduce_scatter | solution.py:59
  111.0 6.9 %copy-start.4 = (bf16[8,2,128,128]{3,0,1,2:T(8,128)(2,1)S(1)}, bf16[8,2,128,128]{3,0,1,2:T(8,128)(2,1)}, u32[]{:S(2)}) copy-start(bf16[8,2,128,128]{3,0,1,2:T(8,128)(2,1)} %fusion.43) | copy-start | bytes 1572868
  137.0 12.4 %copy-start.3 = (bf16[64,256,2]{1,0,2:T(8,128)(2,1)S(1)}, bf16[64,256,2]{1,0,2:T(8,128)(2,1)}, u32[]{:S(2)}) copy-start(bf16[64,256,2]{1,0,2:T(8,128)(2,1)} %fusion.11) | copy-start | bytes 196612
  149.4 5.8 %copy-start = (bf16[128,128,2,128]{3,0,2,1:T(8,128)(2,1)S(1)}, bf16[128,128,2,128]{3,0,2,1:T(8,128)(2,1)}, u32[]{:S(2)}) copy-start(bf16[128,128,2,128]{3,0,2,1:T(8,128)(2,1)} %copy.8) | copy-start | bytes 25165828
Sparse Core Ops, SparseCore 0:
  109.4 9.2 reduce-scatter.4
  158.3 9.2 reduce-scatter.2
where the time goes:
time: 182 us; the launch traced here: 181 us
  local copies, waits for them, and re-layouts  66.4 us (36%)
  matrix products  43.4 us (24%)
  waiting for transfers between devices  41.4 us (23%)
  between operations  14.8 us (8%)
  starting transfers between devices  10.1 us (6%)
  other arithmetic  4.52 us (2%)
    reshape x4, local copies, waits for them, and re-layouts, correlate(): cross_tile = cross_tile.reshape(bin_block, channels, 2, channels)  49.5 us
    ppermute x4, waiting for transfers between devices, from_behind(): return lax.ppermute(x, axis, [(i, (i + by) % size) for i in range(size)])  32 us
    dot_general x4, matrix products, correlate(): jnp.einsum('scfi,scfj->fij', left_part, right_part, preferred_element_typ...  27.4 us
    dot_general x4, matrix products, correlate(): jnp.einsum('tfk,fikj->tij', table_part, cross_tile, preferred_element_typ...  16.1 us
    ppermute x4, starting transfers between devices, from_behind(): return lax.ppermute(x, axis, [(i, (i + by) % size) for i in range(size)])  9.86 us
    reduce_scatter x2, waiting for transfers between devices, per_device(): lax.psum_scatter(partial_lags.astype(jnp.bfloat16), 'sub', scatter_dimens...  9.38 us
    dot_general x4, local copies, waits for them, and re-layouts, correlate(): jnp.einsum('scfi,scfj->fij', left_part, right_part, preferred_element_typ...  6.73 us
    broadcast_in_dim x1, local copies, waits for them, and re-layouts, per_device(): return reduced[:, None]  4.44 us
  transfers between devices with their start and end apart: 6, of which 3 were waited for; matrix products, arithmetic and copies ran while one was open for 57% of the time, Pallas kernels for 0%

commit v1 on v0

v1 whole, which is shorter than its diff:
```python
import math

import jax
import jax.numpy as jnp
from jax import lax
from jax.sharding import PartitionSpec as P

LAGS = 64
ROUNDS = 2


def from_behind(x, axis, by):
    size = lax.axis_size(axis)
    return lax.ppermute(x, axis, [(i, (i + by) % size) for i in range(size)])


def make_table(bin_count, windows, lag_count):
    lags = jnp.arange(lag_count, dtype=jnp.int32) - lag_count // 2
    bins = jnp.arange(bin_count, dtype=jnp.int32)
    period = 2 * bin_count
    phase = bins[None, :] * ((lags[:, None] + period) % period) % period
    angle = phase.astype(jnp.float32) * (math.pi / bin_count)
    weight = (bin_count * windows) ** (-0.5)
    return (jnp.stack([jnp.cos(angle), -jnp.sin(angle)], axis=-1) * weight).astype(jnp.bfloat16)


def correlate(left, partner, flat_table):
    bin_count, channels = partner.shape[2], partner.shape[3]
    cross = jnp.einsum("dscfi,scfk->fdik", left, partner, preferred_element_type=jnp.float32)
    cross = cross.astype(jnp.bfloat16).reshape(bin_count * 2, channels, channels)
    return jnp.einsum("tx,xik->tik", flat_table, cross, preferred_element_type=jnp.float32)


def per_device(spectra, direction):
    windows, _, bin_count, channels = spectra.shape
    lag_table = make_table(bin_count, windows * lax.axis_size("sub"), LAGS)
    flat_table = lag_table.reshape(LAGS, bin_count * 2)
    real, imag = spectra[:, 0], spectra[:, 1]
    left = jnp.stack(
        [jnp.stack([real, imag], axis=1), jnp.stack([-imag, real], axis=1)], axis=0
    )
    reduced_rounds = []
    for round_index in range(ROUNDS):
        ahead = from_behind(spectra, "blk", -(round_index + 1))
        behind = from_behind(spectra, "blk", round_index + 1)
        partner = jnp.where(direction[round_index, 0] == 1, ahead, behind)
        partial_lags = correlate(left, partner, flat_table)
        reduced_rounds.append(
            lax.psum_scatter(
                partial_lags.astype(jnp.bfloat16), "sub", scatter_dimension=0, tiled=True
            ).astype(jnp.float32)
        )
    reduced = jnp.stack(reduced_rounds, axis=0)
    return reduced[:, None]


def solution(mesh):
    return jax.shard_map(
        per_device,
        mesh=mesh,
        in_specs=(P("sub", None, None, ("grp", "blk")), P(None, "blk")),
        out_specs=P(None, ("grp", "blk"), "sub", None, None),
        check_vma=False,
    )
```

time: 182 us -> 181 us (level)
  local copies, waits for them, and re-layouts: 66.4 us -> 5.77 us
  waiting for transfers between devices: 41.4 us -> 93.1 us
  matrix products: 43.4 us -> 53.5 us
    ppermute x4, waiting for transfers between devices: 32 us -> 83.4 us  [from_behind(): return lax.ppermute(x, axis, [(i, (i + by) % size) for i in range(size)])]
    reshape x4 -> x0, local copies, waits for them, and re-layouts: 49.5 us -> none  [correlate(): cross_tile = cross_tile.reshape(bin_block, channels, 2, channels)]
    dot_general x8 -> x4, matrix products: 43.4 us -> 53.5 us  [the longest x2 34 us: correlate(): jnp.einsum('tx,xik->tik', flat_table, cross, preferred_element_type=jnp.f...]
    dot_general x4 -> x0, local copies, waits for them, and re-layouts: 6.73 us -> none  [correlate(): jnp.einsum('scfi,scfj->fij', left_part, right_part, preferred_element_typ...]
    unnamed x15 -> x2, local copies, waits for them, and re-layouts: 4.32 us -> 0.03 us
  transfers between devices with their start and end apart: 6 -> 6, of which waited for: 3 -> 5; matrix products, arithmetic and copies ran while one was open for 57% -> 17% of each run, Pallas kernels for 0% -> 0%
where the time goes in v1:
time: 181 us
  waiting for transfers between devices  93.1 us (51%)
  matrix products  53.5 us (30%)
  between operations  14.7 us (8%)
  starting transfers between devices  9.7 us (5%)
  local copies, waits for them, and re-layouts  5.77 us (3%)
  other arithmetic  4.06 us (2%)
    ppermute x4, waiting for transfers between devices, from_behind(): return lax.ppermute(x, axis, [(i, (i + by) % size) for i in range(size)])  83.4 us
    dot_general x2, matrix products, correlate(): jnp.einsum('tx,xik->tik', flat_table, cross, preferred_element_type=jnp.f...  34 us
    dot_general x2, matrix products, correlate(): jnp.einsum('dscfi,scfk->fdik', left, partner, preferred_element_type=jnp....  19.5 us
    reduce_scatter x2, waiting for transfers between devices, per_device(): lax.psum_scatter(partial_lags.astype(jnp.bfloat16), 'sub', scatter_dimens...  9.74 us
    ppermute x4, starting transfers between devices, from_behind(): return lax.ppermute(x, axis, [(i, (i + by) % size) for i in range(size)])  9.65 us
    broadcast_in_dim x1, local copies, waits for them, and re-layouts, per_device(): return reduced[:, None]  4.44 us
  transfers between devices with their start and end apart: 6, of which 5 were waited for; matrix products, arithmetic and copies ran while one was open for 17% of the time, Pallas kernels for 0%

profile of v1, /device:TPU:0, one launch (start us, length us, event | category | flops | bytes accessed | tf_op | source)
XLA Modules:
  0.0 180.8 jit_solution(14934009692903372126)
XLA Ops:
  6.5 0.0 reduce-scatter.3.cloned.1.call-start
  6.5 6.0 %collective-permute-start = (bf16[8,2,256,128]{3,2,1,0:T(8,128)(2,1)}, bf16[8,2,256,128]{3,2,1,0:T(8,128)(2,1)S(1)}, u32[]{:S(2)}, u32[]{:S(2)}) collective-permute-start(bf16[8,2,256,128]{3,2,1,0:T(8,128)(2,1)} %param.2), channel_id=1, source_target_pairs={{0,14},{2,0},{4,2},{6,4},{8,6},{10,8},{12,10},{14,12},{1,15},{3,1}... | collective-permute-start | bytes 3145736 | tf_op jit(solution)/shard_map/ppermute | solution.py:14
  12.6 0.0 collective-permute-start.1
  12.6 1.3 fusion.25
  14.5 0.0 copy-start
  14.6 1.4 slice_negate_fusion
  16.0 0.1 maximum_bitcast_fusion.1
  16.1 0.0 copy-done
  16.1 0.2 pad_maximum_fusion
  16.3 0.3 fusion.17
  16.6 38.7 %collective-permute-done = bf16[8,2,256,128]{3,2,1,0:T(8,128)(2,1)S(1)} collective-permute-done((bf16[8,2,256,128]{3,2,1,0:T(8,128)(2,1)}, bf16[8,2,256,128]{3,2,1,0:T(8,128)(2,1)S(1)}, u32[]{:S(2)}, u32[]{:S(2)}) %collective-permute-start) | collective-permute-done | bytes 1048608 | tf_op jit(solution)/shard_map/ppermute | solution.py:14
  55.4 0.3 collective-permute-done.1
  55.6 0.1 select_bitcast_fusion.1
  55.7 9.8 %fusion.5 = bf16[256,2,128,128,1]{3,2,4,1,0:T(8,128)(2,1)} fusion(bf16[2,8,2,256,128]{4,3,2,1,0:T(8,128)(2,1)S(1)} %pad_maximum_fusion, bf16[8,2,256,128,1]{3,2,1,0,4:T(8,128)(2,1)S(1)} %select_bitcast_fusion.1), kind=kOutput, calls=%fused_computation.11 | convolution fusion | flops 268435456 | bytes 19922944 | tf_op jit(solution)/shard_map/dscfi,scfk->fdik/dot_general | solution.py:29
  65.5 17.0 %bitcast_convert_fusion.5 = bf16[64,128,128]{2,0,1:T(8,128)(2,1)} fusion(bf16[256,2,128,128,1]{3,2,4,1,0:T(8,128)(2,1)} %fusion.5, f32[64,256,1]{1,0,2:T(8,128)S(1)} %get-tuple-element.10, f32[64,256,1]{1,0,2:T(8,128)S(1)} %get-tuple-element.9), kind=kOutput, calls=%fused_computation.5 | convolution fusion | flops 1074888704 | bytes 19005440 | tf_op jit(solution)/shard_map/tx,xik->tik/dot_general | solution.py:31
  82.5 0.0 reduce-scatter.3.cloned.1.call-update
  82.5 0.0 reduce-scatter.5.cloned.1.call-start
  82.6 3.6 %collective-permute-start.2 = (bf16[8,2,256,128]{3,2,1,0:T(8,128)(2,1)S(1)}, bf16[8,2,256,128]{3,2,1,0:T(8,128)(2,1)S(1)}, u32[]{:S(2)}, u32[]{:S(2)}) collective-permute-start(bf16[8,2,256,128]{3,2,1,0:T(8,128)(2,1)S(1)} %copy-done), channel_id=1, source_target_pairs={{0,12},{2,14},{4,0},{6,2},{8,4},{10,6},{12,8},{14,10},{1,13},{3,15... | collective-permute-start | bytes 3145736 | tf_op jit(solution)/shard_map/ppermute | solution.py:14
  86.2 0.0 collective-permute-start.3
  86.8 23.0 %collective-permute-done.2 = bf16[8,2,256,128]{3,2,1,0:T(8,128)(2,1)S(1)} collective-permute-done((bf16[8,2,256,128]{3,2,1,0:T(8,128)(2,1)S(1)}, bf16[8,2,256,128]{3,2,1,0:T(8,128)(2,1)S(1)}, u32[]{:S(2)}, u32[]{:S(2)}) %collective-permute-start.2) | collective-permute-done | bytes 1048608 | tf_op jit(solution)/shard_map/ppermute | solution.py:14
  109.7 21.4 %collective-permute-done.3 = bf16[8,2,256,128]{3,2,1,0:T(8,128)(2,1)S(1)} collective-permute-done((bf16[8,2,256,128]{3,2,1,0:T(8,128)(2,1)S(1)}, bf16[8,2,256,128]{3,2,1,0:T(8,128)(2,1)S(1)}, u32[]{:S(2)}, u32[]{:S(2)}) %collective-permute-start.3) | collective-permute-done | bytes 1048608 | tf_op jit(solution)/shard_map/ppermute | solution.py:14
  131.1 0.1 select_bitcast_fusion
  131.2 9.8 %fusion.3 = bf16[256,2,128,128,1]{3,2,4,1,0:T(8,128)(2,1)} fusion(bf16[2,8,2,256,128]{4,3,2,1,0:T(8,128)(2,1)S(1)} %pad_maximum_fusion, bf16[8,2,256,128,1]{3,2,1,0,4:T(8,128)(2,1)S(1)} %select_bitcast_fusion), kind=kOutput, calls=%fused_computation.9 | convolution fusion | flops 268435456 | bytes 19922944 | tf_op jit(solution)/shard_map/dscfi,scfk->fdik/dot_general | solution.py:29
  141.0 17.0 %bitcast_convert_fusion.4 = bf16[64,128,128]{2,0,1:T(8,128)(2,1)} fusion(bf16[256,2,128,128,1]{3,2,4,1,0:T(8,128)(2,1)} %fusion.3, f32[64,256,1]{1,0,2:T(8,128)S(1)} %get-tuple-element.10, f32[64,256,1]{1,0,2:T(8,128)S(1)} %get-tuple-element.9), kind=kOutput, calls=%fused_computation.4 | convolution fusion | flops 1074888704 | bytes 19005440 | tf_op jit(solution)/shard_map/tx,xik->tik/dot_general | solution.py:31
  158.0 0.0 reduce-scatter.5.cloned.1.call-update
  158.0 0.0 reduce-scatter.3.cloned.1.call-done
  158.0 9.7 %reduce-scatter.5.cloned.1.call-done = bf16[32,128,128]{2,0,1:T(8,128)(2,1)} async-done(((bf16[64,128,128]{2,0,1:T(8,128)(2,1)}), bf16[32,128,128]{2,0,1:T(8,128)(2,1)}) %reduce-scatter.5.cloned.1.call-update) | async-done | bytes 1048592 | tf_op jit(solution)/shard_map/reduce_scatter | solution.py:49
  167.7 1.8 %fusion.2 = f32[2,1,32,128,128]{4,2,3,0,1:T(8,128)S(1)} fusion(bf16[1,32,128,128]{3,1,2,0:T(8,128)(2,1)} %bitcast.38, bf16[1,32,128,128]{3,1,2,0:T(8,128)(2,1)} %bitcast.37), kind=kLoop, calls=%fused_computation.8 | loop fusion | flops 2097152 | bytes 6291456 | tf_op jit(solution)/shard_map/broadcast_in_dim | solution.py:54
  169.5 4.4 %copy.3 = f32[2,1,32,128,128]{4,3,2,1,0:T(8,128)} copy(f32[2,1,32,128,128]{4,2,3,0,1:T(8,128)S(1)} %fusion.2) | data formatting | bytes 8388608 | tf_op jit(solution)/shard_map/broadcast_in_dim | solution.py:54
  (1 shorter events, 0.0 us)
Async XLA Ops:
  6.5 151.5 %reduce-scatter.3.cloned.1.call-start = ((), (), s32[]{:S(2)}) async-start(), calls=%async_computation.2 | async-start | bytes 3145728 | tf_op jit(solution)/shard_map/reduce_scatter | solution.py:49
  6.5 48.8 %collective-permute-start = (bf16[8,2,256,128]{3,2,1,0:T(8,128)(2,1)}, bf16[8,2,256,128]{3,2,1,0:T(8,128)(2,1)S(1)}, u32[]{:S(2)}, u32[]{:S(2)}) collective-permute-start(bf16[8,2,256,128]{3,2,1,0:T(8,128)(2,1)} %param.2), channel_id=1, source_target_pairs={{0,14},{2,0},{4,2},{6,4},{8,6},{10,8},{12,10},{14,12},{1,15},{3,1}... | collective-permute-start | bytes 3145736 | tf_op jit(solution)/shard_map/ppermute | solution.py:14
  12.6 43.1 %collective-permute-start.1 = (bf16[8,2,256,128]{3,2,1,0:T(8,128)(2,1)}, bf16[8,2,256,128]{3,2,1,0:T(8,128)(2,1)S(1)}, u32[]{:S(2)}, u32[]{:S(2)}) collective-permute-start(bf16[8,2,256,128]{3,2,1,0:T(8,128)(2,1)} %param.2), channel_id=1, source_target_pairs={{0,2},{2,4},{4,6},{6,8},{8,10},{10,12},{12,14},{14,0},{1,3},{3,5},... | collective-permute-start | bytes 3145736 | tf_op jit(solution)/shard_map/ppermute | solution.py:14
  14.5 1.5 copy-start
  82.5 85.2 %reduce-scatter.5.cloned.1.call-start = ((), (), s32[]{:S(2)}) async-start(), calls=%async_computation.3 | async-start | bytes 3145728 | tf_op jit(solution)/shard_map/reduce_scatter | solution.py:49
  82.6 27.2 %collective-permute-start.2 = (bf16[8,2,256,128]{3,2,1,0:T(8,128)(2,1)S(1)}, bf16[8,2,256,128]{3,2,1,0:T(8,128)(2,1)S(1)}, u32[]{:S(2)}, u32[]{:S(2)}) collective-permute-start(bf16[8,2,256,128]{3,2,1,0:T(8,128)(2,1)S(1)} %copy-done), channel_id=1, source_target_pairs={{0,12},{2,14},{4,0},{6,2},{8,4},{10,6},{12,8},{14,10},{1,13},{3,15... | collective-permute-start | bytes 3145736 | tf_op jit(solution)/shard_map/ppermute | solution.py:14
  86.2 44.9 %collective-permute-start.3 = (bf16[8,2,256,128]{3,2,1,0:T(8,128)(2,1)S(1)}, bf16[8,2,256,128]{3,2,1,0:T(8,128)(2,1)S(1)}, u32[]{:S(2)}, u32[]{:S(2)}) collective-permute-start(bf16[8,2,256,128]{3,2,1,0:T(8,128)(2,1)S(1)} %copy-done), channel_id=1, source_target_pairs={{0,4},{2,6},{4,8},{6,10},{8,12},{10,14},{12,0},{14,2},{1,5},{3,7},... | collective-permute-start | bytes 3145736 | tf_op jit(solution)/shard_map/ppermute | solution.py:14
Sparse Core Ops, SparseCore 0:
  82.6 11.0 reduce-scatter.2
  158.1 9.5 reduce-scatter.4
